TPU v7x, 32 devices: a whole 2x2x4 slice. The times are simulated.
32 devices in a mesh: gx: 4 (over z), gy: 8 (over y, x, core).
Axes of the slice: x: 2, y: 2, z: 4, core: 2. Of those that a mesh axis runs over, the one named last changes fastest.
Arguments:
- particles: bfloat16 [2048, 4096], P(('gx', 'gy')), may hold values from -6 to 6
- references: bfloat16 [4, 12, 4096], P('gx'), may hold values from -1 to 1
- slot_class: int32 [4], replicated, may hold values from 0 to 3, each once
- log_prior: float32 [4], replicated, may hold values from -2 to 2
- shift_offsets: int32 [8, 2], replicated, may hold values from -8 to 8
- group_ids: int32 [2048], P(('gx', 'gy')), may hold values from 0 to 127
- ctf_table: float32 [128, 2048], replicated, may hold values from -1 to 1
- noise_power: float32 [2048], replicated, may hold values from 0.5 to 2
Outputs:
- class_sums: float32 [4, 12, 4096], P('gx')
- ctf_power: float32 [4, 2048], P('gx')
- log_evidence: float32 [], replicated
Inputs may be any that keep to these rules, and one draw needn't show every extreme that they name: `slot_class`: each class id stands at exactly one slot.
All inputs are finite; a program needn't handle non-finite values.
Results may differ from a plain program's by a relative error of at most 0.006.
Values may be sent and summed in bfloat16 or wider, within the bound.
No kernel may reach another device: no remote copies, remote signals or barrier semaphores. Data moves between devices by JAX's collectives and lax.ppermute only.
A program may use at most 64 MiB of HBM per device.

v0:
```python
import jax
import jax.numpy as jnp
from jax import lax
from jax.sharding import PartitionSpec as P

L = 64
R = 12
NS = 8
G = 128
HALF = 2048
FR = 4096


def phase_tables(shift_offsets, edge_len):
    half_size = edge_len * edge_len // 2
    freq_index = jnp.arange(half_size, dtype=jnp.int32)
    row_freq = freq_index // (edge_len // 2)
    col_freq = freq_index % (edge_len // 2)
    phase_turns = jnp.mod(
        row_freq[None, :] * shift_offsets[:, 0:1] + col_freq[None, :] * shift_offsets[:, 1:2],
        edge_len,
    )
    angles = phase_turns.astype(jnp.float32) * (2.0 * jnp.pi / edge_len)
    return (jnp.cos(angles), jnp.sin(angles))


def spectra(particles, edge_len):
    rows_here = particles.shape[0]
    half_side = edge_len // 2
    images = particles.astype(jnp.float32).reshape(rows_here * edge_len, edge_len)
    pixel_index = jnp.arange(edge_len, dtype=jnp.int32)
    column_turns = jnp.mod(pixel_index[:, None] * pixel_index[None, :half_side], edge_len).astype(
        jnp.float32
    ) * (2.0 * jnp.pi / edge_len)
    column_table = jnp.concatenate([jnp.cos(column_turns), -jnp.sin(column_turns)], axis=1)
    partial_x = jnp.dot(
        images, column_table, precision=lax.Precision.HIGHEST, preferred_element_type=jnp.float32
    )
    partial_x = partial_x.reshape(rows_here, edge_len, edge_len)
    row_turns = jnp.mod(pixel_index[:, None] * pixel_index[None, :], edge_len).astype(
        jnp.float32
    ) * (2.0 * jnp.pi / edge_len)
    with_cos = jnp.einsum(
        "uy,pyw->puw", jnp.cos(row_turns), partial_x, precision=lax.Precision.HIGHEST
    )
    with_sin = jnp.einsum(
        "uy,pyw->puw", jnp.sin(row_turns), partial_x, precision=lax.Precision.HIGHEST
    )
    real_part = (with_cos[..., :half_side] + with_sin[..., half_side:]) / edge_len
    imag_part = (with_cos[..., half_side:] - with_sin[..., :half_side]) / edge_len
    return (real_part.reshape(rows_here, -1), imag_part.reshape(rows_here, -1))


def shards(
    particles, references, slot_class, log_prior, shift_offsets, group_ids, ctf_table, noise_power
):
    rows_here = particles.shape[0]
    classes = lax.axis_size("gx") * references.shape[0]
    row_width = R * NS
    real_part, imag_part = spectra(particles, L)
    inv_noise = 1.0 / noise_power
    group_hot = (group_ids[:, None] == jnp.arange(G, dtype=jnp.int32)[None, :]).astype(jnp.float32)
    ctf_rows = jnp.dot(
        group_hot, ctf_table, precision=lax.Precision.HIGHEST, preferred_element_type=jnp.float32
    )
    whiten = ctf_rows * inv_noise
    weighted = jnp.concatenate([real_part * whiten, imag_part * whiten], axis=1).astype(
        jnp.bfloat16
    )
    data_power = jnp.sum((real_part * real_part + imag_part * imag_part) * inv_noise, axis=1)
    cosines, sine_table = phase_tables(shift_offsets, L)
    power_table = ctf_table * ctf_table * inv_noise
    blank = jnp.zeros((rows_here, classes * row_width), jnp.float32)
    piece = lax.all_gather(references, "gx", axis=0, tiled=True)

    def add_class(offset, table):
        stack_row = lax.dynamic_index_in_dim(piece, offset, 0, keepdims=False).astype(jnp.float32)
        stack_real = stack_row[:, :HALF]
        stack_imag = stack_row[:, HALF:]
        shifted_real = (
            stack_real[:, None, :] * cosines[None] + stack_imag[:, None, :] * sine_table[None]
        )
        shifted_imag = (
            stack_imag[:, None, :] * cosines[None] - stack_real[:, None, :] * sine_table[None]
        )
        shifted = (
            jnp.concatenate([shifted_real, shifted_imag], axis=2)
            .astype(jnp.bfloat16)
            .reshape(row_width, FR)
        )
        intersection = lax.dot_general(
            weighted, shifted, (((1,), (1,)), ((), ())), preferred_element_type=jnp.float32
        )
        amplitude = stack_real * stack_real + stack_imag * stack_imag
        ref_power = jnp.dot(
            power_table,
            amplitude.T,
            precision=lax.Precision.HIGHEST,
            preferred_element_type=jnp.float32,
        )
        own_power = jnp.dot(
            group_hot,
            ref_power,
            precision=lax.Precision.HIGHEST,
            preferred_element_type=jnp.float32,
        )
        logits = intersection.reshape(rows_here, R, NS) - 0.5 * own_power[:, :, None]
        return lax.dynamic_update_slice_in_dim(
            table, logits.reshape(rows_here, row_width), offset * row_width, 1
        )

    scores = lax.fori_loop(0, piece.shape[0], add_class, blank)
    slot_prior = jnp.sum(
        jnp.where(
            slot_class[:, None] == jnp.arange(classes, dtype=jnp.int32)[None, :],
            log_prior[None, :],
            0.0,
        ),
        axis=1,
    )
    logits = (
        scores.reshape(rows_here, classes, row_width)
        - 0.5 * data_power[:, None, None]
        + slot_prior[None, :, None]
    )
    row_max = jnp.max(logits, axis=(1, 2), keepdims=True)
    raised = jnp.exp(logits - row_max)
    normaliser = jnp.sum(raised, axis=(1, 2), keepdims=True)
    weights = raised / normaliser
    evidence = row_max[:, 0, 0] + jnp.log(normaliser[:, 0, 0])
    weights_low = weights.astype(jnp.bfloat16)
    group_weights = jnp.dot(
        jnp.sum(weights, axis=2).T,
        group_hot,
        precision=lax.Precision.HIGHEST,
        preferred_element_type=jnp.float32,
    )

    def class_terms(slot_index):
        weight_cols = lax.dynamic_index_in_dim(weights_low, slot_index, 1, keepdims=False)
        moment = lax.dot_general(
            weight_cols, weighted, (((0,), (0,)), ((), ())), preferred_element_type=jnp.float32
        )
        moment = moment.reshape(R, NS, FR)
        moment_real = moment[..., :HALF]
        moment_imag = moment[..., HALF:]
        back_real = jnp.sum(moment_real * cosines[None] - moment_imag * sine_table[None], axis=1)
        back_imag = jnp.sum(moment_imag * cosines[None] + moment_real * sine_table[None], axis=1)
        return jnp.concatenate([back_real, back_imag], axis=1)

    owned = lax.psum_scatter(
        lax.map(
            lambda offset: class_terms(offset),
            jnp.arange(references.shape[0] * lax.axis_size("gx"), dtype=jnp.int32),
        ),
        "gx",
        scatter_dimension=0,
        tiled=True,
    )
    class_sums = lax.psum(owned, "gy")
    totals, evidence_sum = lax.psum((group_weights, jnp.sum(evidence)), ("gx", "gy"))
    own_groups = lax.dynamic_slice_in_dim(totals, lax.axis_index("gx"), 1, 0)
    ctf_power = jnp.dot(
        own_groups,
        ctf_table * ctf_table,
        precision=lax.Precision.HIGHEST,
        preferred_element_type=jnp.float32,
    )
    log_evidence = evidence_sum / (rows_here * lax.axis_size("gx") * lax.axis_size("gy") * HALF)
    return (class_sums, ctf_power, log_evidence)


def solution(mesh):
    return jax.shard_map(
        shards,
        mesh=mesh,
        in_specs=(
            P(("gx", "gy"), None),
            P("gx", None, None),
            P(),
            P(),
            P(),
            P(("gx", "gy")),
            P(),
            P(),
        ),
        out_specs=(P("gx", None, None), P("gx", None), P()),
        check_vma=False,
    )
```

profile of v0, /device:TPU:0, one launch (start us, length us, event | category | flops | bytes accessed | tf_op | source)
XLA Modules:
  0.0 206.5 jit_solution(13460478304987082292)
XLA Ops:
  7.4 2.1 reshape.111
  9.4 1.3 convolution_bitcast_fusion.1
  10.7 0.8 reshape.112
  11.6 4.6 %fusion.46 = f32[64,64,64]{1,2,0:T(8,128)} fusion(f32[64,64,64]{1,0,2:T(8,128)S(1)} %reshape.112), kind=kOutput, calls=%fused_computation.59 | convolution fusion | flops 201383936 | bytes 2097152 | tf_op jit(solution)/shard_map/uy,pyw->puw/dot_general | solution.py:43
  16.2 4.7 %fusion.49 = f32[64,64,64]{1,2,0:T(8,128)} fusion(f32[64,64,64]{1,0,2:T(8,128)S(1)} %reshape.112), kind=kOutput, calls=%fused_computation.60 | convolution fusion | flops 201383936 | bytes 2097152 | tf_op jit(solution)/shard_map/uy,pyw->puw/dot_general | solution.py:46
  20.9 0.6 fusion.82
  21.7 3.4 %multiply_reduce_fusion = (f32[64]{0:T(128)}, f32[64,64,32]{1,2,0:T(8,128)S(1)}, f32[64,64,32]{1,2,0:T(8,128)S(1)}) fusion(f32[64,32]{0,1:T(8,128)S(1)} %copy.44, f32[64,64,64]{1,2,0:T(8,128)} %fusion.49, f32[64,64,64]{1,2,0:T(8,128)} %fusion.46), kind=kLoop, calls=%fused_computation.65 | loop fusion | flops 1179584 | bytes 3154176 | tf_op jit(solution)/shard_map/reduce_sum | solution.py:70
  25.1 1.1 copy.39
  26.1 1.1 copy.40
  27.3 1.1 copy.41
  28.4 1.1 copy.42
  29.7 0.6 slice_bitcast_fusion
  30.3 18.2 %all_gather.3 = bf16[4,12,4096]{2,1,0:T(8,128)(2,1)} all-gather(bf16[1,12,4096]{2,1,0:T(8,128)(2,1)S(1)} %copy-done.3), channel_id=1, replica_groups=mesh['gx'=4,'gy'=8] {'gx'}, dimensions={0}, use_global_device_ids=true | all-gather | bytes 491520 | tf_op jit(solution)/shard_map/all_gather | solution.py:74
  48.4 1.2 multiply_convert_fusion.1
  49.7 25.9 %while.27 = (s32[]{:T(128)}, f32[64,384]{1,0:T(8,128)S(1)}, bf16[4,12,4096]{2,1,0:T(8,128)(2,1)}, bf16[64,4096]{1,0:T(8,128)(2,1)S(1)}, f32[128,2048]{1,0:T(8,12...) while((s32[]{:T(128)}, f32[64,384]{1,0:T(8,128)S(1)}, ...), condition=%wide.region_1.2_spmd.clone.clone, body=%wide.region_0.1_spmd.clone.clone.sunk | while | flops 92814080 | bytes 4696571 | solution.py:112
  49.7 0.9 bitcast_convert_fusion.2
  50.7 1.1 fusion.137
  52.0 0.9 fusion.135
  52.9 0.9 fusion.136
  53.8 0.7 copy.55
  54.5 1.2 fusion.140
  56.1 0.9 bitcast_convert_fusion.2
  57.1 1.1 fusion.137
  58.4 0.9 fusion.135
  59.3 0.9 fusion.136
  60.2 0.7 copy.55
  60.9 1.2 fusion.140
  62.1 0.6 dynamic_update_slice.18
  62.7 0.9 bitcast_convert_fusion.2
  63.6 1.1 fusion.137
  64.9 0.9 fusion.135
  65.8 0.9 fusion.136
  66.7 0.7 copy.55
  67.4 1.2 fusion.140
  68.6 0.6 dynamic_update_slice.18
  69.2 0.9 bitcast_convert_fusion.2
  70.2 1.1 fusion.137
  71.5 0.9 fusion.135
  72.4 0.9 fusion.136
  73.3 0.7 copy.55
  74.0 1.2 fusion.140
  75.6 0.7 broadcast_multiply_fusion
  76.3 0.9 select_reduce_fusion
  78.0 21.0 %while.28 = (s32[]{:T(128)}, f32[4,12,4096]{2,1,0:T(8,128)}, s32[4]{0:T(128)S(1)}, bf16[64,4,96]{0,2,1:T(8,128)(2,1)S(1)}, bf16[64,4096]{1,0:T(8,128)(2,1)S(1)},...) while((s32[]{:T(128)}, f32[4,12,4096]{2,1,0:T(8,128)}, ...), condition=%wide.region_9.10_spmd.clone.clone, body=%wide.region_6.9_spmd.clone.clone.sunk | while | flops 52166660 | bytes 4629223 | solution.py:152
  78.0 0.6 dynamic_slice.40
  80.9 1.1 fusion.144
  82.0 0.6 subtract_reduce_fusion.2
  82.5 0.7 fusion.145
  83.2 0.6 dynamic_slice.40
  86.1 1.1 fusion.144
  87.8 0.7 fusion.145
  88.5 0.6 dynamic_slice.40
  91.4 1.1 fusion.144
  93.0 0.7 fusion.145
  93.7 0.6 dynamic_slice.40
  96.6 1.1 fusion.144
  97.7 0.6 subtract_reduce_fusion.2
  98.3 0.7 fusion.145
  99.1 0.6 add_reduce_fusion.1
  99.7 0.8 fusion.68
  100.5 42.4 %all-reduce = (f32[4,128]{1,0:T(4,128)S(1)}, f32[]{:T(128)}) all-reduce(f32[4,128]{1,0:T(4,128)S(1)} %fusion.68, f32[]{:T(128)} %add_reduce_fusion.1), channel_id=1, replica_groups=mesh['gx'=4,'gy'=8] {'gx','gy'}, use_global_device_ids=true, to_apply=%region_13.14 | all-reduce | flops 513 | bytes 4104 | tf_op jit(solution)/shard_map/psum | solution.py:161
  143.0 1.2 fusion.54
  144.9 51.8 %all-reduce.3.cloned.1.call-done = f32[1,12,4096]{2,1,0:T(8,128)} async-done(((f32[1,12,4096]{2,1,0:T(8,128)}), f32[1,12,4096]{2,1,0:T(8,128)}) %all-reduce.3.cloned.1.call-update) | async-done | bytes 196624 | tf_op jit(solution)/shard_map/psum | solution.py:160
  196.7 1.8 copy.45
  (53 shorter events, 5.8 us)
Async XLA Ops:
  7.2 135.8 %reduce-scatter.2.cloned.1.call-start = ((), (), s32[]{:S(2)}) async-start(), calls=%async_computation.1 | async-start | bytes 1310720 | tf_op jit(solution)/shard_map/reduce_scatter | solution.py:151
  16.2 5.3 %copy-start.4 = (f32[2048]{0:T(1024)S(1)}, f32[2048]{0:T(1024)}, u32[]{:S(2)}) copy-start(f32[2048]{0:T(1024)} %param.19) | copy-start | bytes 24580
  27.3 2.3 %copy-start = (f32[128,2048]{1,0:T(8,128)S(1)}, f32[128,2048]{1,0:T(8,128)}, u32[]{:S(2)}) copy-start(f32[128,2048]{1,0:T(8,128)} %param.18) | copy-start | bytes 3145732
  28.4 1.3 copy-start.5
  28.4 1.9 copy-start.3
  29.5 18.9 %copy-start.1 = (f32[64,2048]{1,0:T(8,128)S(1)}, f32[64,2048]{1,0:T(8,128)}, u32[]{:S(2)}) copy-start(f32[64,2048]{1,0:T(8,128)} %copy.40) | copy-start | bytes 1572868
  29.5 18.9 %copy-start.2 = (f32[64,2048]{1,0:T(8,128)S(1)}, f32[64,2048]{1,0:T(8,128)}, u32[]{:S(2)}) copy-start(f32[64,2048]{1,0:T(8,128)} %copy.42) | copy-start | bytes 1572868
  99.0 97.7 %all-reduce.3.cloned.1.call-start = ((), (), s32[]{:S(2)}) async-start(), calls=%async_computation.2 | async-start | bytes 524288 | tf_op jit(solution)/shard_map/psum | solution.py:160
Sparse Core Ops, SparseCore 0:
  99.2 29.8 reduce-scatter.1
  143.1 53.5 all-reduce.2
where the time goes:
time: 208 us; the launch traced here: 206 us
  blocking collectives  60.6 us (29%)
  waiting for transfers between devices  51.9 us (25%)
  matrix products  27.2 us (13%)
  other arithmetic  25.1 us (12%)
  local copies, waits for them, and re-layouts  17.6 us (8%)
  between operations  16 us (8%)
  loops' own time  8.13 us (4%)
    psum x1, waiting for transfers between devices, shards(): class_sums = lax.psum(owned, 'gy')  51.8 us
    psum x1, blocking collectives, shards(): lax.psum((group_weights, jnp.sum(evidence)), ('gx', 'gy'))  42.4 us
    all_gather x1, blocking collectives, shards(): piece = lax.all_gather(references, 'gx', axis=0, tiled=True)  18.2 us
    cos x8, other arithmetic, phase_tables(): return (jnp.cos(angles), jnp.sin(angles))  8.53 us
    another operation x1, loops' own time, shards(): lax.map(lambda offset: class_terms(offset), jnp.arange(references.shape[0...  7.85 us
    dot_general x1, matrix products, spectra(): jnp.einsum('uy,pyw->puw', jnp.sin(row_turns), partial_x, precision=lax.Pr...  4.7 us
    dot_general x1, matrix products, spectra(): jnp.einsum('uy,pyw->puw', jnp.cos(row_turns), partial_x, precision=lax.Pr...  4.65 us
    dot_general x4, matrix products, add_class(): lax.dot_general(weighted, shifted, (((1,), (1,)), ((), ())), preferred_el...  4.62 us
  transfers between devices with their start and end apart: 2, of which 1 were waited for; matrix products, arithmetic and copies ran while one was open for 1% of the time, Pallas kernels for 0%

commit v1 on v0

--- a/solution.py
+++ b/solution.py
@@ -9,6 +9,28 @@
 G = 128
 HALF = 2048
 FR = 4096
+
+
+def laid_out(tiles, dim):
+    lengths = list(tiles.shape[1:])
+    lengths[dim] *= tiles.shape[0]
+    return jnp.moveaxis(tiles, 0, dim).reshape(lengths)
+
+
+def grow_blocks(x, axis):
+    peers = lax.axis_size(axis)
+    parts = x[None]
+    for level in range(peers.bit_length() - 1):
+        distance = 1 << level
+        other = lax.ppermute(parts, axis, [(i, i ^ distance) for i in range(peers)])
+        both = jnp.stack([parts, other])
+        upper = lax.axis_index(axis) >> level & 1
+        parts = jnp.where(upper == 0, both, both[::-1]).reshape(-1, *x.shape)
+    return parts
+
+
+def doubled_up(shard, axis, dim):
+    return laid_out(grow_blocks(shard, axis), dim)
 
 
 def phase_tables(shift_offsets, edge_len):
@@ -71,7 +93,7 @@
     cosines, sine_table = phase_tables(shift_offsets, L)
     power_table = ctf_table * ctf_table * inv_noise
     blank = jnp.zeros((rows_here, classes * row_width), jnp.float32)
-    piece = lax.all_gather(references, "gx", axis=0, tiled=True)
+    piece = doubled_up(references, "gx", 0)
 
     def add_class(offset, table):
         stack_row = lax.dynamic_index_in_dim(piece, offset, 0, keepdims=False).astype(jnp.float32)

time: 208 us -> 208 us (level)
  blocking collectives: 60.6 us -> 40.5 us
  waiting for transfers between devices: 51.9 us -> 62.9 us
  starting transfers between devices: 0.08 us -> 5.85 us
    all_gather x1 -> x0, blocking collectives: 18.2 us -> none  [shards(): piece = lax.all_gather(references, 'gx', axis=0, tiled=True)]
    ppermute x0 -> x2, waiting for transfers between devices: none -> 11 us  [grow_blocks(): other = lax.ppermute(parts, axis, [(i, i ^ distance) for i in range(peers)])]
    ppermute x0 -> x2, starting transfers between devices: none -> 5.77 us  [grow_blocks(): other = lax.ppermute(parts, axis, [(i, i ^ distance) for i in range(peers)])]
  transfers between devices with their start and end apart: 2 -> 4, of which waited for: 1 -> 2; matrix products, arithmetic and copies ran while one was open for 1% -> 13% of each run, Pallas kernels for 0% -> 0%
where the time goes in v1:
time: 208 us; the launch traced here: 206 us
  waiting for transfers between devices  62.9 us (30%)
  blocking collectives  40.5 us (19%)
  matrix products  27.3 us (13%)
  other arithmetic  26.7 us (13%)
  local copies, waits for them, and re-layouts  18.7 us (9%)
  between operations  16 us (8%)
  loops' own time  8.12 us (4%)
  starting transfers between devices  5.85 us (3%)
    psum x1, waiting for transfers between devices, shards(): class_sums = lax.psum(owned, 'gy')  51.9 us
    psum x1, blocking collectives, shards(): lax.psum((group_weights, jnp.sum(evidence)), ('gx', 'gy'))  40.5 us
    ppermute x2, waiting for transfers between devices, grow_blocks(): other = lax.ppermute(parts, axis, [(i, i ^ distance) for i in range(peers)])  11 us
    cos x8, other arithmetic, phase_tables(): return (jnp.cos(angles), jnp.sin(angles))  8.53 us
    another operation x1, loops' own time, shards(): lax.map(lambda offset: class_terms(offset), jnp.arange(references.shape[0...  7.85 us
    ppermute x2, starting transfers between devices, grow_blocks(): other = lax.ppermute(parts, axis, [(i, i ^ distance) for i in range(peers)])  5.77 us
    dot_general x1, matrix products, spectra(): jnp.einsum('uy,pyw->puw', jnp.sin(row_turns), partial_x, precision=lax.Pr...  4.7 us
    dot_general x1, matrix products, spectra(): jnp.einsum('uy,pyw->puw', jnp.cos(row_turns), partial_x, precision=lax.Pr...  4.65 us
  transfers between devices with their start and end apart: 4, of which 2 were waited for; matrix products, arithmetic and copies ran while one was open for 13% of the time, Pallas kernels for 0%

profile of v1, /device:TPU:0, one launch (start us, length us, event | category | flops | bytes accessed | tf_op | source)
XLA Modules:
  0.0 206.2 jit_solution(4508169425790653852)
XLA Ops:
  7.2 3.1 %collective-permute-start = (bf16[1,1,12,4096]{3,2,1,0:T(8,128)(2,1)}, bf16[1,1,12,4096]{3,2,1,0:T(8,128)(2,1)S(1)}, u32[]{:S(2)}, u32[]{:S(2)}) collective-permute-start(bf16[1,1,12,4096]{3,2,1,0:T(8,128)(2,1)} %bitcast.100), channel_id=1, source_target_pairs={{0,8},{8,0},{16,24},{24,16},{1,9},{9,1},{17,25},{25,17},{2,10},{10... | collective-permute-start | bytes 294920 | tf_op jit(solution)/shard_map/ppermute | solution.py:25
  10.5 2.1 reshape.115
  12.6 1.3 convolution_bitcast_fusion.1
  13.8 0.8 reshape.116
  14.7 4.7 %fusion.46 = f32[64,64,64]{1,2,0:T(8,128)} fusion(f32[64,64,64]{1,0,2:T(8,128)S(1)} %reshape.116), kind=kOutput, calls=%fused_computation.59 | convolution fusion | flops 201383936 | bytes 2097152 | tf_op jit(solution)/shard_map/uy,pyw->puw/dot_general | solution.py:65
  19.3 4.7 %fusion.49 = f32[64,64,64]{1,2,0:T(8,128)} fusion(f32[64,64,64]{1,0,2:T(8,128)S(1)} %reshape.116), kind=kOutput, calls=%fused_computation.60 | convolution fusion | flops 201383936 | bytes 2097152 | tf_op jit(solution)/shard_map/uy,pyw->puw/dot_general | solution.py:68
  24.2 2.8 %multiply_reduce_fusion = (f32[64]{0:T(128)S(1)}, f32[64,64,32]{1,2,0:T(8,128)S(1)}, f32[64,64,32]{1,2,0:T(8,128)S(1)}) fusion(f32[64,32]{0,1:T(8,128)S(1)} %copy.44, f32[64,64,64]{1,2,0:T(8,128)} %fusion.49, f32[64,64,64]{1,2,0:T(8,128)} %fusion.46), kind=kLoop, calls=%fused_computation.65 | loop fusion | flops 1179584 | bytes 3154176 | tf_op jit(solution)/shard_map/reduce_sum | solution.py:92
  27.0 1.1 copy.39
  28.1 1.1 copy.40
  29.2 1.1 copy.41
  30.3 1.1 copy.42
  33.0 0.7 add.146
  33.7 1.4 multiply_convert_fusion.1
  35.1 0.6 fusion.84
  35.8 2.7 %collective-permute-start.1 = (bf16[2,1,12,4096]{3,2,0,1:T(8,128)(2,1)S(1)}, bf16[2,1,12,4096]{3,2,0,1:T(8,128)(2,1)S(1)}, u32[]{:S(2)}, u32[]{:S(2)}) collective-permute-start(bf16[2,1,12,4096]{3,2,0,1:T(8,128)(2,1)S(1)} %get-tuple-element.382), channel_id=1, source_target_pairs={{0,16},{8,24},{16,0},{24,8},{1,17},{9,25},{17,1},{25,9},{2,18},{10... | collective-permute-start | bytes 589832 | tf_op jit(solution)/shard_map/ppermute | solution.py:25
  39.0 11.0 %collective-permute-done.1 = bf16[2,1,12,4096]{3,2,0,1:T(8,128)(2,1)S(1)} collective-permute-done((bf16[2,1,12,4096]{3,2,0,1:T(8,128)(2,1)S(1)}, bf16[2,1,12,4096]{3,2,0,1:T(8,128)(2,1)S(1)}, u32[]{:S(2)}, u32[]{:S(2)}) %collective-permute-start.1) | collective-permute-done | bytes 196640 | tf_op jit(solution)/shard_map/ppermute | solution.py:25
  50.1 0.9 reverse_select_fusion
  50.9 25.9 %while.27 = (s32[]{:T(128)}, f32[64,384]{1,0:T(8,128)S(1)}, bf16[4,12,4096]{2,1,0:T(8,128)(2,1)}, bf16[64,4096]{1,0:T(8,128)(2,1)S(1)}, f32[128,2048]{1,0:T(8,12...) while((s32[]{:T(128)}, f32[64,384]{1,0:T(8,128)S(1)}, ...), condition=%wide.region_1.2_spmd.clone.clone, body=%wide.region_0.1_spmd.clone.clone.sunk | while | flops 92814080 | bytes 4696571 | solution.py:134
  51.0 0.9 bitcast_convert_fusion.2
  51.9 1.1 fusion.139
  53.2 0.9 fusion.137
  54.1 0.9 fusion.138
  55.0 0.7 copy.55
  55.7 1.2 fusion.142
  57.4 0.9 bitcast_convert_fusion.2
  58.3 1.1 fusion.139
  59.6 0.9 fusion.137
  60.5 0.9 fusion.138
  61.4 0.7 copy.55
  62.1 1.2 fusion.142
  63.3 0.6 dynamic_update_slice.18
  63.9 0.9 bitcast_convert_fusion.2
  64.9 1.1 fusion.139
  66.1 0.9 fusion.137
  67.1 0.9 fusion.138
  68.0 0.7 copy.55
  68.7 1.2 fusion.142
  69.8 0.6 dynamic_update_slice.18
  70.5 0.9 bitcast_convert_fusion.2
  71.4 1.1 fusion.139
  72.7 0.9 fusion.137
  73.6 0.9 fusion.138
  74.5 0.7 copy.55
  75.2 1.2 fusion.142
  77.0 0.9 fusion.58
  77.9 0.9 exponential_reduce_fusion
  78.8 0.8 fusion.103
  79.6 21.0 %while.28 = (s32[]{:T(128)}, f32[4,12,4096]{2,1,0:T(8,128)}, s32[4]{0:T(128)S(1)}, bf16[64,4,96]{0,2,1:T(8,128)(2,1)S(1)}, bf16[64,4096]{1,0:T(8,128)(2,1)S(1)},...) while((s32[]{:T(128)}, f32[4,12,4096]{2,1,0:T(8,128)}, ...), condition=%wide.region_9.10_spmd.clone.clone, body=%wide.region_6.9_spmd.clone.clone.sunk | while | flops 52166660 | bytes 4629223 | solution.py:174
  79.6 0.6 dynamic_slice.40
  82.5 1.1 fusion.146
  84.1 0.7 fusion.147
  87.7 1.1 fusion.146
  89.3 0.7 fusion.147
  90.1 0.6 dynamic_slice.40
  93.0 1.1 fusion.146
  94.6 0.7 fusion.147
  98.2 1.1 fusion.146
  99.8 0.7 fusion.147
  100.7 0.6 add_reduce_fusion.1
  101.3 0.8 fusion.70
  102.1 40.5 %all-reduce = (f32[4,128]{1,0:T(4,128)S(1)}, f32[]{:T(128)}) all-reduce(f32[4,128]{1,0:T(4,128)S(1)} %fusion.70, f32[]{:T(128)} %add_reduce_fusion.1), channel_id=1, replica_groups=mesh['gx'=4,'gy'=8] {'gx','gy'}, use_global_device_ids=true, to_apply=%region_13.14 | all-reduce | flops 513 | bytes 4104 | tf_op jit(solution)/shard_map/psum | solution.py:183
  142.6 1.2 fusion.54
  144.5 51.9 %all-reduce.3.cloned.1.call-done = f32[1,12,4096]{2,1,0:T(8,128)} async-done(((f32[1,12,4096]{2,1,0:T(8,128)}), f32[1,12,4096]{2,1,0:T(8,128)}) %all-reduce.3.cloned.1.call-update) | async-done | bytes 196624 | tf_op jit(solution)/shard_map/psum | solution.py:182
  196.4 1.8 copy.45
  (66 shorter events, 9.4 us)
Async XLA Ops:
  7.2 135.4 %reduce-scatter.2.cloned.1.call-start = ((), (), s32[]{:S(2)}) async-start(), calls=%async_computation.1 | async-start | bytes 1310720 | tf_op jit(solution)/shard_map/reduce_scatter | solution.py:173
  7.2 28.5 %collective-permute-start = (bf16[1,1,12,4096]{3,2,1,0:T(8,128)(2,1)}, bf16[1,1,12,4096]{3,2,1,0:T(8,128)(2,1)S(1)}, u32[]{:S(2)}, u32[]{:S(2)}) collective-permute-start(bf16[1,1,12,4096]{3,2,1,0:T(8,128)(2,1)} %bitcast.100), channel_id=1, source_target_pairs={{0,8},{8,0},{16,24},{24,16},{1,9},{9,1},{17,25},{25,17},{2,10},{10... | collective-permute-start | bytes 294920 | tf_op jit(solution)/shard_map/ppermute | solution.py:25
  19.3 4.7 %copy-start.4 = (f32[2048]{0:T(1024)S(1)}, f32[2048]{0:T(1024)}, u32[]{:S(2)}) copy-start(f32[2048]{0:T(1024)} %param.19) | copy-start | bytes 24580
  29.2 2.3 %copy-start = (f32[128,2048]{1,0:T(8,128)S(1)}, f32[128,2048]{1,0:T(8,128)}, u32[]{:S(2)}) copy-start(f32[128,2048]{1,0:T(8,128)} %param.18) | copy-start | bytes 3145732
  30.3 1.3 copy-start.6
  30.3 1.9 copy-start.7
  30.3 1.8 copy-start.8
  30.3 3.3 %copy-start.1 = (f32[64,2048]{1,0:T(8,128)S(1)}, f32[64,2048]{1,0:T(8,128)}, u32[]{:S(2)}) copy-start(f32[64,2048]{1,0:T(8,128)} %copy.40) | copy-start | bytes 1572868
  31.5 2.2 %copy-start.2 = (f32[64,2048]{1,0:T(8,128)S(1)}, f32[64,2048]{1,0:T(8,128)}, u32[]{:S(2)}) copy-start(f32[64,2048]{1,0:T(8,128)} %copy.42) | copy-start | bytes 1572868
  31.6 4.1 %copy-start.3 = (bf16[1,12,4096]{2,1,0:T(8,128)(2,1)S(1)}, bf16[1,12,4096]{2,1,0:T(8,128)(2,1)}, u32[]{:S(2)}) copy-start(bf16[1,12,4096]{2,1,0:T(8,128)(2,1)} %param.13) | copy-start | bytes 294916
  32.3 0.6 copy-start.5
  35.8 14.2 %collective-permute-start.1 = (bf16[2,1,12,4096]{3,2,0,1:T(8,128)(2,1)S(1)}, bf16[2,1,12,4096]{3,2,0,1:T(8,128)(2,1)S(1)}, u32[]{:S(2)}, u32[]{:S(2)}) collective-permute-start(bf16[2,1,12,4096]{3,2,0,1:T(8,128)(2,1)S(1)} %get-tuple-element.382), channel_id=1, source_target_pairs={{0,16},{8,24},{16,0},{24,8},{1,17},{9,25},{17,1},{25,9},{2,18},{10... | collective-permute-start | bytes 589832 | tf_op jit(solution)/shard_map/ppermute | solution.py:25
  100.6 95.8 %all-reduce.3.cloned.1.call-start = ((), (), s32[]{:S(2)}) async-start(), calls=%async_computation.2 | async-start | bytes 524288 | tf_op jit(solution)/shard_map/psum | solution.py:182
Sparse Core Ops, SparseCore 0:
  100.7 28.2 reduce-scatter.1
  142.7 53.6 all-reduce.2
